TPU v7x, 32 devices: a whole 2x2x4 slice. The times are simulated.
32 devices in a mesh: leaf: 8 (over z, y), row: 4 (over x, core).
Axes of the slice: x: 2, y: 2, z: 4, core: 2. Of those that a mesh axis runs over, the one named last changes fastest.
Arguments:
- panel0: float32 [12288, 512], P(('leaf', 'row')), may hold values from -3 to 30, as said below
- panel1: float32 [6144, 512], P(('leaf', 'row')), may hold values from -3 to 30
- panel2: float32 [3072, 512], P(('leaf', 'row')), may hold values from -3 to 30
- panel3: float32 [1536, 512], P(('leaf', 'row')), may hold values from -3 to 30
- maps1: int32 [8, 8], replicated, may hold values from 0 to 11, as said below
- maps2: int32 [4, 8], replicated, may hold values from 0 to 11, as said below
- maps3: int32 [2, 8], replicated, may hold values from 0 to 11, as said below
Outputs:
- update_top: float32 [1024, 1024], P(('leaf', 'row'))
Inputs may be any that keep to these rules, and one draw needn't show every extreme that they name: `panel0`: each front's first 512 rows form a symmetric matrix, and every assembled pivot block is positive definite. `maps1`: each row lists distinct parent block numbers. `maps2`: each row lists distinct parent block numbers. `maps3`: each row lists distinct parent block numbers.
All inputs are finite; a program needn't handle non-finite values.
Results may differ from a plain program's by a relative error of at most 0.0003.
Values sent between devices are 32-bit elements; how exact they have to be, the bound alone decides.
A program may use at most 128 MiB of HBM per device.

v0:
```python
import functools
import math

import jax
import jax.numpy as jnp
from jax import lax
from jax.experimental import pallas as pl
from jax.experimental.pallas import tpu as pltpu
from jax.sharding import PartitionSpec as P

BLOCK = 128
SUB = 8
LEVELS = 4
CONTRACT_LAST = (((1,), (1,)), ((), ()))
CONTRACT_FIRST = (((1,), (0,)), ((), ()))


def halves(value):
    high = value.astype(jnp.bfloat16)
    low = (value - high.astype(jnp.float32)).astype(jnp.bfloat16)
    return high, low


def dot_split(left, right):
    left_high, left_low = left
    right_high, right_low = right

    def one(a, b):
        return lax.dot_general(a, b, CONTRACT_LAST, preferred_element_type=jnp.float32)

    return one(left_high, right_high) + (one(left_high, right_low) + one(left_low, right_high))


def dot_nt(left, right):
    return dot_split(halves(left), halves(right))


def spread(value, rows, columns):
    return jnp.broadcast_to(value, (rows, columns))


def diagonal_inverse(block, pause):
    count = BLOCK // SUB
    rows = [block[v * SUB : (v + 1) * SUB] for v in range(count)]
    lane = lax.broadcasted_iota(jnp.int32, (SUB, BLOCK), 1)
    sub = lax.broadcasted_iota(jnp.int32, (SUB, BLOCK), 0)
    for b in range(count):
        if b == count // 2:
            pause()
        base = b * SUB
        inside = (lane >= base) & (lane < base + SUB)
        own = rows[b]
        columns = [spread(own[:, base + j : base + j + 1], SUB, BLOCK) for j in range(SUB)]
        a = [
            [spread(columns[j][i : i + 1], SUB, BLOCK) for j in range(i + 1)] for i in range(SUB)
        ]
        inverse = []
        ratio = [[None] * SUB for _ in range(SUB)]
        for i in range(SUB):
            inverse.append(1.0 / a[i][i])
            for j in range(i + 1, SUB):
                ratio[j][i] = a[j][i] * inverse[i]
            for j in range(i + 1, SUB):
                for k in range(i + 1, j + 1):
                    a[j][k] = a[j][k] - ratio[j][i] * a[k][i]
        cleared = jnp.where(inside, 0.0, own)
        pivots = []
        for j in range(SUB):
            row = spread(cleared[j : j + 1], SUB, BLOCK)
            row = jnp.where(lane == base + j, 1.0, row)
            for i in range(j):
                row = row - ratio[j][i] * pivots[i]
            pivots.append(row)
        for v in range(b + 1, count):
            old = rows[v]
            new = jnp.where(inside, 0.0, old)
            factors = []
            for j in range(SUB):
                column = spread(old[:, base + j : base + j + 1], SUB, BLOCK)
                for i in range(j):
                    column = column - factors[i] * a[j][i]
                factors.append(column * inverse[j])
            for j in range(SUB):
                new = new - factors[j] * pivots[j]
            rows[v] = new
        final = jnp.zeros((SUB, BLOCK), jnp.float32)
        scale = jnp.ones((SUB, BLOCK), jnp.float32)
        for j in range(SUB):
            final = jnp.where(sub == j, pivots[j], final)
            scale = jnp.where(sub == j, a[j][j], scale)
        rows[b] = jnp.where(lane <= sub + base, final / jnp.sqrt(scale), 0.0)
    return jnp.concatenate(rows, axis=0)


def neighbours(level):
    leaf = lax.axis_index("leaf")
    row = lax.axis_index("row")
    partners = []
    for bit in range(level):
        flag = leaf // 2**bit % 2
        partners.append({"leaf": leaf + (1 - 2 * flag) * 2**bit, "row": row})
    count = lax.axis_size("row")
    sibling = row + 1 - 2 * (row % 2)
    forward = [lax.rem(row + 2 * d, count) for d in range(1, count // 2)]
    backward = [lax.rem(row + count - 2 * d, count) for d in range(1, count // 2)]
    across = [{"leaf": leaf, "row": other} for other in forward]
    return partners, {"leaf": leaf, "row": sibling}, across, backward


def remote(source, target, sends, receives, slot, device):
    return pltpu.make_async_remote_copy(
        src_ref=source,
        dst_ref=target,
        send_sem=sends.at[slot],
        recv_sem=receives.at[slot],
        device_id=device,
        device_id_type=pl.DeviceIdType.MESH,
    )


class Gather:
    def __init__(self, buffer, place, sends, receives, slot, near, source=None):
        _, sibling, across, origins = near
        own = buffer.at[place(lax.axis_index("row"))]
        if source is None:
            source = own
        self.direct = remote(source, own, sends, receives, slot, sibling)
        self.far = []
        self.relay = []
        for n, (device, origin) in enumerate(zip(across, origins)):
            self.far.append(remote(source, own, sends, receives, slot + 1 + 2 * n, device))
            passed = buffer.at[place(origin)]
            self.relay.append(remote(passed, passed, sends, receives, slot + 2 + 2 * n, sibling))

    def start(self):
        for copy in self.far:
            copy.start()
        self.direct.start()

    def pass_on(self):
        for copy, relay in zip(self.far, self.relay):
            copy.wait_recv()
            relay.start()

    def finish(self):
        self.direct.wait_recv()
        for relay in self.relay:
            relay.wait_recv()
        for copy in [self.direct] + self.far + self.relay:
            copy.wait_send()


def rows_at(size, base=0):
    def place(row):
        return pl.ds(pl.multiple_of(row * size + base, 8), size)

    return place


def column_tiles(order):
    count = order // BLOCK
    return [(i, j) for j in range(count) for i in range(j, count)]


def pivot_chunks(order):
    count = order // BLOCK
    return [(0, 1), (1, count), (count, 2 * count - 1), (2 * count - 1, len(column_tiles(order)))]


def dot_split_nn(left, right):
    left_high, left_low = left
    right_high, right_low = right

    def one(a, b):
        return lax.dot_general(a, b, CONTRACT_FIRST, preferred_element_type=jnp.float32)

    return one(left_high, right_high) + (one(left_high, right_low) + one(left_low, right_high))


def entry_barrier(near):
    partners, sibling, across, _ = near
    barrier = pltpu.get_barrier_semaphore()
    peers = partners + [sibling] + across
    for peer in peers:
        pl.semaphore_signal(barrier, inc=1, device_id=peer, device_id_type=pl.DeviceIdType.MESH)
    pl.semaphore_wait(barrier, len(peers))


def bit_reversed(index, bits):
    return sum((index >> b & 1) << (bits - 1 - b) for b in range(bits))


def rows_at_scaled(stride, base, size):
    def place(row):
        return pl.ds(pl.multiple_of(row * stride + base, 8), size)

    return place


class Links:
    def __init__(self, near, sends, receives):
        self.near = near
        self.sends = sends
        self.receives = receives
        self.used = 0

    def copy(self, source, target, device):
        slot = self.used
        self.used += 1
        return remote(source, target, self.sends, self.receives, slot, device)

    def gather(self, buffer, place, source=None):
        slot = self.used
        self.used += 1 + 2 * len(self.near[2])
        return Gather(buffer, place, self.sends, self.receives, slot, self.near, source)


def gather_task(move):
    return [move.start, move.pass_on, move.finish]


def sum_task(links, bits, share, start, height, inbox, sums, target, stride, base):
    row = lax.axis_index("row")
    partners = links.near[0]
    span = pl.ds(start, height)
    place = rows_at_scaled(stride, base, height)
    moves = []
    for k, bit in enumerate(bits):
        source = share.at[span] if k == 0 else sums.at[k - 1, span]
        moves.append(links.copy(source, inbox.at[k, span], partners[bit]))
    spread = links.gather(target, place)

    def advance(k):
        moves[k].wait()
        total = (share[span] if k == 0 else sums[k - 1, span]) + inbox[k, span]
        if k + 1 < len(bits):
            sums[k, span] = total
            moves[k + 1].start()
        else:
            target[place(row)] = total
            spread.start()

    steps = [functools.partial(advance, k) for k in range(len(bits))]
    return [moves[0].start] + steps + [spread.pass_on, spread.finish]


def scatter_task(links, bits, share, start, height, inbox, sums, target, stride):
    row = lax.axis_index("row")
    leaf = lax.axis_index("leaf")
    partners = links.near[0]
    flags = [leaf // 2**bit % 2 for bit in bits]
    heights = [height // 2 ** (k + 1) for k in range(len(bits))]
    moves = []
    for k, bit in enumerate(bits):
        size = heights[k]
        other = pl.multiple_of((1 - flags[k]) * size, 8)
        if k == 0:
            source = share.at[pl.ds(start + other, size)]
        else:
            source = sums.at[k - 1, pl.ds(other, size)]
        moves.append(links.copy(source, inbox.at[k, pl.ds(0, size)], partners[bit]))
    regions = []
    origin = row * stride + start
    for flag, size in zip(flags, heights):
        origin = origin + flag * size
        regions.append(pl.ds(pl.multiple_of(origin, 8), size))
    returns = []
    for region, bit in reversed(list(zip(regions, bits))):
        returns.append(links.copy(target.at[region], target.at[region], partners[bit]))
    spread = links.gather(target, rows_at_scaled(stride, start, height))

    def reduce(k):
        size = heights[k]
        moves[k].wait()
        keep = pl.multiple_of(flags[k] * size, 8)
        mine = share[pl.ds(start + keep, size)] if k == 0 else sums[k - 1, pl.ds(keep, size)]
        total = mine + inbox[k, :size]
        if k + 1 < len(bits):
            sums[k, :size] = total
            moves[k + 1].start()
        else:
            target[regions[-1]] = total
            returns[0].start()

    def widen(k):
        returns[k].wait()
        if k + 1 < len(bits):
            returns[k + 1].start()
        else:
            spread.start()

    down = [functools.partial(reduce, k) for k in range(len(bits))]
    up = [functools.partial(widen, k) for k in range(len(bits))]
    return [moves[0].start] + down + up + [spread.pass_on, spread.finish]


def extra_task(links, bits, extra, columns, inbox, middle, final_in, result):
    leaf = lax.axis_index("leaf")
    partners = links.near[0]
    flags = [leaf // 2**bit % 2 for bit in range(LEVELS - 1)]
    size = result.shape[0]
    near, far = bits[0], bits[1]

    def pick(axis, flag):
        return (pl.ds(flag, 1), pl.ds(0, 2)) if axis == 0 else (pl.ds(0, 2), pl.ds(flag, 1))

    def inner(flag):
        return (pl.ds(0, 1), pl.ds(flag, 1)) if near == 0 else (pl.ds(flag, 1), pl.ds(0, 1))

    deep = LEVELS - 2
    half = lambda flag: pl.ds(pl.multiple_of(flag * size, 8), size)
    whole = pl.ds(0, 2 * size)
    give = extra.at[(*pick(near, 1 - flags[near]), whole, columns)]
    moves = [links.copy(give, inbox, partners[near])]
    moves.append(links.copy(middle.at[0].at[inner(1 - flags[far])], middle.at[1].at[(pl.ds(0, 1), pl.ds(0, 1))], partners[far]))
    moves.append(links.copy(final_in.at[0, half(1 - flags[deep])], final_in.at[1, pl.ds(0, size)], partners[deep]))

    def one():
        moves[0].wait()
        middle[0] = extra[(*pick(near, flags[near]), whole, columns)] + inbox[...]
        moves[1].start()

    def two():
        moves[1].wait()
        kept = middle[(0, *inner(flags[far]))] + middle[1, :1, :1]
        final_in[0] = kept.reshape(kept.shape[2:])
        moves[2].start()

    def three():
        moves[2].wait()
        result[...] = final_in[0, half(flags[deep])] + final_in[1, :size]

    return [moves[0].start, one, two, three]


def factor(diagonal, column, lower, inverse, spare, hook):
    order = lower.shape[1]
    tiles = order // BLOCK
    product, cross, block = spare
    row_ids = lax.broadcasted_iota(jnp.int32, (order, BLOCK), 0)

    def store(target, where, value):
        high, low = halves(value)
        target[(0, *where)] = high
        target[(1, *where)] = low

    def step(j, carry):
        hook(j, 0)
        start = pl.multiple_of(j * BLOCK, BLOCK)
        span = pl.ds(start, BLOCK)
        mine = lower[0, span], lower[1, span]
        product[...] = dot_split((lower[0], lower[1]), mine)
        cross[...] = dot_split_nn(mine, (inverse[0], inverse[1]))
        block[...] = diagonal_inverse(
            diagonal(j) - dot_split(mine, mine), functools.partial(hook, j, 1)
        )
        hook(j, 2)
        own = halves(block[...])
        below = jnp.where(row_ids >= start + BLOCK, column(j) - product[...], 0.0)
        store(lower, (slice(None), span), dot_split(halves(below), own))
        store(inverse, (span, slice(None)), -dot_split_nn(own, halves(cross[...])))
        inverse[0, span, span] = own[0]
        inverse[1, span, span] = own[1]
        return carry

    lax.fori_loop(0, tiles, step, 0)


def front_kernel(level, row_count, front, order, *refs):
    last = level == LEVELS - 1
    first = level == 0
    group = 2**level
    below = front - order
    refs = list(refs)
    take = lambda: refs.pop(0)
    row = lax.axis_index("row")
    member = lax.axis_index("leaf") % group
    panels = joined = ()
    if first:
        panel, *panels = take(), take()
    else:
        pivot_share, below_share = take(), take()
    if level == 1:
        panels = [take() for _ in range(LEVELS - 2)]
    if last:
        extra = take()
    result = take()
    joined = [take() for _ in panels]
    lower, inverse, product, cross, block, columns, sends, receives = [take() for _ in range(8)]
    held = [take() for _ in panels]
    near = neighbours(level)
    links = Links(near, sends, receives)
    lower[...] = jnp.zeros_like(lower)
    inverse[...] = jnp.zeros_like(inverse)
    entry_barrier(near)
    panel_tasks = []
    for part, buffer in zip(panels, held):
        size = part.shape[0]
        panel_tasks.append(gather_task(links.gather(buffer, rows_at(size), part)))
        buffer[rows_at(size)(row)] = part[...]
    if first:
        gathered = take()
        chunk = panel.shape[0]

        def piece(base, size, left, width):
            def place(index):
                return rows_at_scaled(chunk, base, size)(index), pl.ds(left, width)

            source = panel.at[pl.ds(base, size), pl.ds(left, width)]
            return gather_task(links.gather(gathered, place, source))

        step = math.gcd(chunk, BLOCK)
        strips = [piece(base, step, 0, BLOCK) for base in range(0, chunk, step)]
        strips += [piece(0, chunk, left, BLOCK) for left in range(BLOCK, order, BLOCK)]
        for strip in strips:
            strip[0]()
        own = pl.ds(pl.multiple_of(row * chunk, 8), chunk)
        gathered[own] = panel[...]
        panel_tasks[0][0]()
        lead = chunk // step
        early = BLOCK // step
        for stage in (1, 2):
            for strip in strips[:early]:
                strip[stage]()
        rest = strips[early:lead]
        plan = {(0, 1): [s[1] for s in rest], (0, 2): [s[2] for s in rest]}
        for n, strip in enumerate(strips[lead:]):
            plan[n, 2] = plan.get((n, 2), []) + [strip[1]]
            plan[n + 1, 0] = [strip[2]]
        after = panel_tasks[0][1:]

        def diagonal(j):
            span = pl.ds(pl.multiple_of(j * BLOCK, BLOCK), BLOCK)
            return gathered[span, span]

        def column(j):
            return gathered[:order, pl.ds(pl.multiple_of(j * BLOCK, BLOCK), BLOCK)]

    else:
        packed, pivot_sum, pivot_in, below_sum, below_in = [take() for _ in range(5)]
        tasks = []
        turns = [list(range(level)), list(range(level))]
        if level > 1:
            turns[1][0], turns[1][1] = 1, 0
        for n, (begin, end) in enumerate(pivot_chunks(order)):
            size = BLOCK // row_count
            height = (end - begin) * size
            bits = turns[n % 2] if n else turns[0]
            tasks.append(
                sum_task(
                    links, bits, pivot_share, begin * size, height, pivot_in, pivot_sum,
                    packed, height, begin * BLOCK,
                )
            )
        share = below_share.shape[0]
        for n in range(2):
            height = share // 2
            if last:
                tasks.append(
                    scatter_task(
                        links, turns[n], below_share, n * height, height, below_in.at[n],
                        below_sum.at[n], columns, share,
                    )
                )
            else:
                tasks.append(
                    sum_task(
                        links, turns[n], below_share, n * height, height, below_in, below_sum,
                        columns, share, n * height,
                    )
                )
        a, b, c, d, e, f = tasks
        both = lambda k: [e[k], f[k]]
        pre = [t[0] for t in tasks]
        if level == 1:
            pre += [a[1], b[1], a[2], c[1], d[1]] + [t[0] for t in panel_tasks] + [b[2], a[3]]
            plan = {
                (0, 1): [c[2], d[2]],
                (0, 2): [b[3]],
                (1, 0): [c[3], e[1]],
                (1, 1): [d[3]],
                (2, 1): [f[1]] + [t[1] for t in panel_tasks],
                (3, 0): [e[2]],
                (3, 1): [e[3]] + [t[2] for t in panel_tasks],
            }
            after = [f[2], f[3]]
        elif level == 2:
            pre += [a[1], b[1], c[1], d[1], a[2], b[2], c[2], d[2], a[3], b[3], a[4]]
            plan = {
                (0, 1): [c[3], d[3]] + both(1),
                (0, 2): [b[4]],
                (1, 0): [c[4]],
                (1, 1): [d[4]],
                (2, 0): both(2),
                (3, 1): [e[3]],
                (3, 2): [e[4]],
            }
            after = [f[3], f[4]]
        else:
            inbox0, middle0, final0, inbox1, middle1, final1, sums0, sums1 = [take() for _ in range(8)]
            half = below // 2
            x = extra_task(links, (0, 1), extra, pl.ds(0, half), inbox0, middle0, final0, sums0)
            y = extra_task(links, (1, 0), extra, pl.ds(half, half), inbox1, middle1, final1, sums1)
            pre += [a[1], b[1], c[1], d[1], a[2], b[2], c[2], d[2]] + both(1) + [x[0], y[0]]
            pre += [a[3], b[3], a[4], c[3], d[3], b[4], a[5]]
            plan = {
                (0, 1): both(2) + [c[4], d[4]],
                (0, 2): [b[5]],
                (1, 0): [c[5]] + both(3),
                (1, 1): [x[1], y[1]] + both(4),
                (2, 0): [d[5]] + both(5),
                (2, 1): [x[2], y[2]],
                (2, 2): both(6),
                (3, 1): [x[3], y[3]],
                (3, 2): [e[7]],
            }
            after = [f[7], e[8], f[8]]
        for action in pre:
            action()

        count = order // BLOCK

        def diagonal(j):
            place = j * count - j * (j - 1) // 2
            return packed[pl.ds(pl.multiple_of(place * BLOCK, BLOCK), BLOCK)]

        def column(j):
            place = j * count - j * (j - 1) // 2 - j
            return packed[pl.ds(pl.multiple_of(place * BLOCK, BLOCK), order)]

    def hook(j, slot):
        for (when, which), actions in plan.items():
            if which == slot:

                @pl.when(j == when)
                def _():
                    for action in actions:
                        action()

    factor(diagonal, column, lower, inverse, (product, cross, block), hook)
    for action in after:
        action()
    if last:
        height = result.shape[0]
        position = member * row_count + row
        own = columns[pl.ds(pl.multiple_of(position * height, 8), height)]
        whole = inverse[0], inverse[1]
        weight = dot_split_nn(halves(dot_split(halves(own), whole)), whole)
        rest = dot_nt(weight, columns[...])
        result[:, :half] = sums0[...] - rest[:, :half]
        result[:, half:] = sums1[...] - rest[:, half:]
        return
    width = order // group
    if first:
        for left in range(0, order, 2 * BLOCK):
            right = min(left + 2 * BLOCK, order)
            part = inverse[0, left:right, :right], inverse[1, left:right, :right]
            result[:, left:right] = dot_split(halves(gathered[order:, :right]), part)
    else:
        span = pl.ds(pl.multiple_of(member * width, BLOCK), width)
        result[...] = dot_split(halves(columns[...]), (inverse[0, span], inverse[1, span]))
    for buffer, target in zip(held, joined):
        target[...] = buffer[...]


def share_kernel(level, row_count, front, order, *refs):
    group = 2**level
    below = front - order
    refs = list(refs)
    take = lambda: refs.pop(0)
    inverse_map, next_panel, fresh = take(), take(), take()
    old = take() if level else None
    kept, pivot_out, below_out = take(), take(), take()
    extra = take() if level == LEVELS - 2 else None
    placed, whole_panel, everything = take(), take(), take()
    row = lax.axis_index("row")
    depth = 0 if old is None else old.shape[1]
    width = order // group
    if old is not None:
        kept[:below, :depth] = old[:below]
    kept[:below, depth:] = fresh[...]
    kept[below:] = jnp.zeros((BLOCK, depth + width), jnp.float32)
    for i in range(front // BLOCK):
        block = pl.multiple_of(inverse_map[i] * BLOCK, BLOCK)
        placed[i * BLOCK : (i + 1) * BLOCK] = kept[pl.ds(block, BLOCK)]
    held = next_panel.shape[0]
    whole_panel[...] = jnp.zeros_like(whole_panel)
    place = lax.axis_index("leaf") % (2 * group)
    whole_panel[pl.ds(pl.multiple_of(place * held, 8), held)] = next_panel[...]
    pivots = halves(placed[:order])
    for t, (i, j) in enumerate(column_tiles(order)):
        down = slice(i * BLOCK, (i + 1) * BLOCK)
        along = slice(j * BLOCK, (j + 1) * BLOCK)
        product = dot_split([p[down] for p in pivots], [p[along] for p in pivots])
        everything[t * BLOCK : (t + 1) * BLOCK] = whole_panel[down, along] - product
    for begin, end in pivot_chunks(order):
        size = BLOCK // row_count
        height = (end - begin) * size
        mine = rows_at_scaled(height, begin * BLOCK, height)(row)
        pivot_out[begin * size : end * size] = everything[mine]
    height = below_out.shape[0]
    mine = rows_at_scaled(height, order, height)(row)
    below_out[...] = whole_panel[mine] - dot_split(halves(placed[mine]), pivots)
    kept[:below] = placed[order:]
    if level == LEVELS - 2:
        top = 2 * group
        height = below // (top * row_count)
        for index in range(top):
            start = pl.multiple_of(order + (index * row_count + row) * height, 8)
            spot = bit_reversed(index, LEVELS - 1)
            placed[spot * height : (spot + 1) * height] = placed[pl.ds(start, height)]
        own_part = halves(placed[: top * height])
        value = -dot_split(own_part, halves(kept[:below]))
        extra[...] = value.reshape(extra.shape)


def front_step(level, row_count, front, order, operands):
    below = front - order
    width = order // 2**level
    share = len(column_tiles(order)) * BLOCK // row_count
    float32 = jnp.float32

    def vmem(*shape, dtype=float32):
        return pltpu.VMEM(shape, dtype)

    def out(*shape):
        return jax.ShapeDtypeStruct(shape, float32)

    last = level == LEVELS - 1
    rest = below // row_count
    top = 2 ** (LEVELS - 1)
    copies = 8 * (row_count - 1) + 32
    scratch = [
        vmem(2, order, order, dtype=jnp.bfloat16),
        vmem(2, order, order, dtype=jnp.bfloat16),
        vmem(order, BLOCK),
        vmem(BLOCK, order),
        vmem(BLOCK, BLOCK),
        vmem(below if level else 8, order),
        pltpu.SemaphoreType.DMA((copies,)),
        pltpu.SemaphoreType.DMA((copies,)),
    ]
    panels = operands[1:] if level == 0 else operands[2:] if level == 1 else []
    heights = [row_count * panel.shape[0] for panel in panels]
    scratch += [vmem(height, order) for height in heights]
    if level == 0:
        scratch.append(vmem(front, order))
    else:
        scratch += [
            vmem(share * row_count, BLOCK),
            vmem(level, share, BLOCK),
            vmem(level, share, BLOCK),
        ]
        if last:
            scratch += [vmem(2, level, rest // 4, order), vmem(2, level, rest // 4, order)]
        else:
            scratch += [vmem(level, rest, order), vmem(level, rest, order)]
    if last:
        height = rest // top
        half = below // 2
        for shape in ((1, 2), (2, 1)):
            scratch += [
                vmem(*shape, 2 * height, half),
                vmem(2, *shape, 2 * height, half),
                vmem(2, 2 * height, half),
            ]
        scratch += [vmem(height, half), vmem(height, half)]
        shapes = out(height, below)
    else:
        shapes = [out(below, width)] + [out(height, order) for height in heights]
    specs = [pl.BlockSpec(memory_space=pltpu.VMEM)] * len(operands)
    return pl.pallas_call(
        functools.partial(front_kernel, level, row_count, front, order),
        out_shape=shapes,
        in_specs=specs,
        scratch_shapes=scratch,
        name=f"front{level}",
        compiler_params=pltpu.CompilerParams(
            vmem_limit_bytes=60 * 2**20, collective_id=level, has_side_effects=True
        ),
    )(*operands)


def share_step(level, row_count, front, order, operands):
    below = front - order
    depth = sum(order // 2**k for k in range(level + 1))
    tiles = len(column_tiles(order))
    rest = below // row_count

    def out(*shape):
        return jax.ShapeDtypeStruct(shape, jnp.float32)

    shapes = [out(below + BLOCK, depth), out(tiles * BLOCK // row_count, BLOCK), out(rest, order)]
    if level == LEVELS - 2:
        shapes.append(out(2, 2, rest // 4, below))
    specs = [pl.BlockSpec(memory_space=pltpu.VMEM)] * len(operands)
    specs[0] = pl.BlockSpec(memory_space=pltpu.SMEM)
    return pl.pallas_call(
        functools.partial(share_kernel, level, row_count, front, order),
        out_shape=shapes,
        in_specs=specs,
        scratch_shapes=[
            pltpu.VMEM((front, depth), jnp.float32),
            pltpu.VMEM((front, order), jnp.float32),
            pltpu.VMEM((tiles * BLOCK, BLOCK), jnp.float32),
        ],
        name=f"share{level}",
        compiler_params=pltpu.CompilerParams(vmem_limit_bytes=60 * 2**20),
    )(*operands)


def body(panel0, panel1, panel2, panel3, maps1, maps2, maps3):
    block_maps = (maps1, maps2, maps3)
    row_count = lax.axis_size("row")
    leaf = lax.axis_index("leaf")
    order = panel0.shape[1]
    front = panel0.shape[0] * row_count
    parents = front // BLOCK
    children = (front - order) // BLOCK
    operands = [panel0, panel1]
    waiting = [[], [panel2, panel3], []]
    old = []
    panels = []
    for level in range(LEVELS - 1):
        blocks = lax.dynamic_index_in_dim(block_maps[level], leaf // 2**level, 0, keepdims=False)
        hit = blocks[None, :] == jnp.arange(parents, dtype=jnp.int32)[:, None]
        back = jnp.min(
            jnp.where(hit, jnp.arange(children, dtype=jnp.int32)[None, :], children), axis=1
        )
        fresh, *joined = front_step(level, row_count, front, order, operands + waiting[level])
        panels += joined
        shared = [back, panels[level], fresh] + old
        outs = share_step(level, row_count, front, order, shared)
        old = [outs[0]]
        operands = list(outs[1:])
    return front_step(LEVELS - 1, row_count, front, order, operands)


def solution(mesh):
    rows = P(("leaf", "row"), None)
    return jax.shard_map(
        body,
        mesh=mesh,
        in_specs=(rows, rows, rows, rows, P(), P(), P()),
        out_specs=rows,
        check_vma=False,
    )
```

profile of v0, /device:TPU:0, one launch (start us, length us, event | category | flops | bytes accessed | tf_op | source)
XLA Modules:
  0.0 205.9 jit_solution(3838719181877946438)
XLA Ops:
  0.0 0.0 copy-start
  0.0 0.7 fusion
  0.7 0.6 select_reduce_fusion.2.refs_0_
  1.3 0.7 fusion.2
  2.0 0.6 select_reduce_fusion.refs_0_
  2.5 0.0 copy-done
  2.6 0.6 select_reduce_fusion.1.refs_0_
  3.2 38.7 %front0.1 = (f32[1024,512]{1,0:T(8,128)}, f32[768,512]{1,0:T(8,128)}) custom-call(f32[384,512]{1,0:T(8,128)} %refs_0_.1, f32[192,512]{1,0:T(8,128)} %refs_1_.1), custom_call_target="tpu_custom_call" | custom-call | tf_op jit(solution)/shard_map/front0/pallas_call | solution.py:672
  41.9 5.9 %share0.1 = (f32[1152,512]{1,0:T(8,128)}, f32[320,128]{1,0:T(8,128)}, f32[256,512]{1,0:T(8,128)}) custom-call(s32[12]{0:T(128)} %select_reduce_fusion.1.refs_0_, f32[768,512]{1,0:T(8,128)} %get-tuple-element.19.refs_1_, f32[1024,512]{1,0:T(8,128)} %get-tuple-element.20.refs_2_), custom_call_target="tpu_custom_call" | custom-call | tf_op jit(solution)/shard_map/share0/pallas_call | solution.py:698
  47.8 37.4 %front1.1 = (f32[1024,256]{1,0:T(8,128)}, f32[384,512]{1,0:T(8,128)}, f32[192,512]{1,0:T(8,128)}) custom-call(f32[320,128]{1,0:T(8,128)} %get-tuple-element.21.refs_0_, f32[256,512]{1,0:T(8,128)} %get-tuple-element.22.refs_1_, f32[96,512]{1,0:T(8,128)} %refs_2_.1, f32[48,512]{1,0:T(8,128)} %refs_3_.1), custom_call_target="tpu_custom_call" | custom-call | tf_op jit(solution)/shard_map/front1/pallas_call | solution.py:672
  85.2 7.0 %share1.1 = (f32[1152,768]{1,0:T(8,128)}, f32[320,128]{1,0:T(8,128)}, f32[256,512]{1,0:T(8,128)}) custom-call(s32[12]{0:T(128)} %select_reduce_fusion.refs_0_, f32[384,512]{1,0:T(8,128)} %get-tuple-element.24.refs_1_, f32[1024,256]{1,0:T(8,128)} %get-tuple-element.25.refs_2_, f32[1152,512]{1,0:T(8,128)} %get-tuple-element.26.refs_3_), custom_call_target="tpu_custom_call" | custom-call | tf_op jit(solution)/shard_map/share1/pallas_call | solution.py:698
  92.1 45.5 %front2.1.refs_2_ = f32[1024,128]{1,0:T(8,128)} custom-call(f32[320,128]{1,0:T(8,128)} %get-tuple-element.27.refs_0_, f32[256,512]{1,0:T(8,128)} %get-tuple-element.28.refs_1_), custom_call_target="tpu_custom_call" | custom-call | tf_op jit(solution)/shard_map/front2/pallas_call | solution.py:672
  137.7 9.6 %share2.1 = (f32[1152,896]{1,0:T(8,128)}, f32[320,128]{1,0:T(8,128)}, f32[256,512]{1,0:T(8,128)}, f32[2,2,64,1024]{3,2,1,0:T(8,128)}) custom-call(s32[12]{0:T(128)} %select_reduce_fusion.2.refs_0_, f32[192,512]{1,0:T(8,128)} %get-tuple-element.23.refs_1_, f32[1024,128]{1,0:T(8,128)} %front2.1.refs_2_, f32[1152,768]{1,0:T(8,128)} %get-tuple-element.29.refs_3_), custom_call_target="tpu_custom_call" | custom-call | tf_op jit(solution)/shard_map/share2/pallas_call | solution.py:698
  147.3 57.0 %front3.1 = f32[32,1024]{1,0:T(8,128)} custom-call(f32[320,128]{1,0:T(8,128)} %get-tuple-element.30.refs_0_, f32[256,512]{1,0:T(8,128)} %get-tuple-element.31.refs_1_, f32[2,2,64,1024]{3,2,1,0:T(8,128)} %get-tuple-element.32.refs_2_), custom_call_target="tpu_custom_call" | custom-call | tf_op jit(solution)/shard_map/front3/pallas_call | solution.py:672
  204.4 1.6 copy.9
  (1 shorter events, 0.0 us)
Async XLA Ops:
  0.0 2.5 %copy-start = (s32[8,8]{1,0:T(8,128)S(1)}, s32[8,8]{1,0:T(8,128)}, u32[]{:S(2)}) copy-start(s32[8,8]{1,0:T(8,128)} %param.11) | copy-start | bytes 772
where the time goes:
time: 206 us
  Pallas kernels  201 us (98%)
  local copies, waits for them, and re-layouts  2.96 us (1%)
    pallas_call x4, Pallas kernels, front_step(): pl.pallas_call(functools.partial(front_kernel, level, row_count, front, o...  179 us
    pallas_call x3, Pallas kernels, share_step(): pl.pallas_call(functools.partial(share_kernel, level, row_count, front, o...  22.5 us

commit v1 on v0

--- a/solution.py
+++ b/solution.py
@@ -219,11 +219,9 @@
     return [move.start, move.pass_on, move.finish]
 
 
-def sum_task(links, bits, share, start, height, inbox, sums, target, stride, base):
+def sum_task(links, bits, share, span, inbox, sums, target, place):
     row = lax.axis_index("row")
     partners = links.near[0]
-    span = pl.ds(start, height)
-    place = rows_at_scaled(stride, base, height)
     moves = []
     for k, bit in enumerate(bits):
         source = share.at[span] if k == 0 else sums.at[k - 1, span]
@@ -371,20 +369,22 @@
     first = level == 0
     group = 2**level
     below = front - order
+    count = order // BLOCK
+    size = BLOCK // row_count
     refs = list(refs)
     take = lambda: refs.pop(0)
     row = lax.axis_index("row")
     member = lax.axis_index("leaf") % group
-    panels = joined = ()
+    old = kept = None
     if first:
         panel, *panels = take(), take()
     else:
-        pivot_share, below_share = take(), take()
-    if level == 1:
-        panels = [take() for _ in range(LEVELS - 2)]
-    if last:
-        extra = take()
+        back, next_panel, fresh = take(), take(), take()
+        old = take() if level > 1 else None
+        panels = [take() for _ in range(LEVELS - 2)] if level == 1 else []
     result = take()
+    if not first and not last:
+        kept = take()
     joined = [take() for _ in panels]
     lower, inverse, product, cross, block, columns, sends, receives = [take() for _ in range(8)]
     held = [take() for _ in panels]
@@ -392,21 +392,21 @@
     links = Links(near, sends, receives)
     lower[...] = jnp.zeros_like(lower)
     inverse[...] = jnp.zeros_like(inverse)
-    entry_barrier(near)
     panel_tasks = []
     for part, buffer in zip(panels, held):
-        size = part.shape[0]
-        panel_tasks.append(gather_task(links.gather(buffer, rows_at(size), part)))
-        buffer[rows_at(size)(row)] = part[...]
+        height = part.shape[0]
+        panel_tasks.append(gather_task(links.gather(buffer, rows_at(height), part)))
+        buffer[rows_at(height)(row)] = part[...]
     if first:
+        entry_barrier(near)
         gathered = take()
         chunk = panel.shape[0]
 
-        def piece(base, size, left, width):
+        def piece(base, height, left, width):
             def place(index):
-                return rows_at_scaled(chunk, base, size)(index), pl.ds(left, width)
-
-            source = panel.at[pl.ds(base, size), pl.ds(left, width)]
+                return rows_at_scaled(chunk, base, height)(index), pl.ds(left, width)
+
+            source = panel.at[pl.ds(base, height), pl.ds(left, width)]
             return gather_task(links.gather(gathered, place, source))
 
         step = math.gcd(chunk, BLOCK)
@@ -427,7 +427,9 @@
         for n, strip in enumerate(strips[lead:]):
             plan[n, 2] = plan.get((n, 2), []) + [strip[1]]
             plan[n + 1, 0] = [strip[2]]
-        after = panel_tasks[0][1:]
+        plan[count - 1, 2] = [panel_tasks[0][1]]
+        after = []
+        finally_ = panel_tasks[0][2:]
 
         def diagonal(j):
             span = pl.ds(pl.multiple_of(j * BLOCK, BLOCK), BLOCK)
@@ -437,24 +439,26 @@
             return gathered[:order, pl.ds(pl.multiple_of(j * BLOCK, BLOCK), BLOCK)]
 
     else:
-        packed, pivot_sum, pivot_in, below_sum, below_in = [take() for _ in range(5)]
+        packed, pivot_share, pivot_sum, pivot_in = [take() for _ in range(4)]
+        below_share, below_sum, below_in, placed, whole_panel = [take() for _ in range(5)]
         tasks = []
         turns = [list(range(level)), list(range(level))]
         if level > 1:
             turns[1][0], turns[1][1] = 1, 0
         for n, (begin, end) in enumerate(pivot_chunks(order)):
-            size = BLOCK // row_count
-            height = (end - begin) * size
+
+            def place(index, begin=begin, end=end):
+                return pl.ds(begin, end - begin), pl.ds(pl.multiple_of(index * size, 8), size)
+
             bits = turns[n % 2] if n else turns[0]
+            span = pl.ds(begin, end - begin)
             tasks.append(
-                sum_task(
-                    links, bits, pivot_share, begin * size, height, pivot_in, pivot_sum,
-                    packed, height, begin * BLOCK,
-                )
+                sum_task(links, bits, pivot_share, span, pivot_in, pivot_sum, packed, place)
             )
         share = below_share.shape[0]
-        for n in range(2):
-            height = share // 2
+        parts = 2 if last else 4
+        height = share // parts
+        for n in range(parts):
             if last:
                 tasks.append(
                     scatter_task(
@@ -465,43 +469,99 @@
             else:
                 tasks.append(
                     sum_task(
-                        links, turns[n], below_share, n * height, height, below_in, below_sum,
-                        columns, share, n * height,
+                        links, turns[n % 2], below_share, pl.ds(n * height, height), below_in,
+                        below_sum, columns, rows_at_scaled(share, n * height, height),
                     )
                 )
-        a, b, c, d, e, f = tasks
+        a, b, c, d, e, f, *more = tasks
         both = lambda k: [e[k], f[k]]
-        pre = [t[0] for t in tasks]
+
+        def fetch(i):
+            target = slice(i * BLOCK, (i + 1) * BLOCK)
+            depth = 0 if old is None else old.shape[2]
+            if depth:
+                placed[target, :depth] = old[back[i]]
+            placed[target, depth:] = fresh[back[i]]
+
+        whole_panel[...] = jnp.zeros_like(whole_panel)
+        held_rows = next_panel.shape[0]
+        whole_panel[pl.ds(pl.multiple_of(member * held_rows, 8), held_rows)] = next_panel[...]
+        for i in range(front // BLOCK):
+            fetch(i)
+        entry_barrier(near)
+        pivots = halves(placed[:order])
+        mine = [pl.ds(pl.multiple_of(i * BLOCK + row * size, 8), size) for i in range(count)]
+        own = halves(jnp.concatenate([placed[span] for span in mine], axis=0))
+        part = dot_split(own, pivots)
+        for t, (i, j) in enumerate(column_tiles(order)):
+            along = slice(j * BLOCK, (j + 1) * BLOCK)
+            pivot_share[t] = whole_panel[mine[i], along] - part[i * size : (i + 1) * size, along]
+        for task in (a, b, c, d):
+            task[0]()
+        spot = rows_at_scaled(share, order, share)(row)
+        below_share[...] = whole_panel[spot] - dot_split(halves(placed[spot]), pivots)
+        for task in [e, f] + more:
+            task[0]()
+
+        def keep():
+            kept[: below // BLOCK] = placed[order:].reshape(below // BLOCK, *kept.shape[1:])
+            kept[below // BLOCK] = jnp.zeros(kept.shape[1:], jnp.float32)
+
+        finally_ = []
         if level == 1:
-            pre += [a[1], b[1], a[2], c[1], d[1]] + [t[0] for t in panel_tasks] + [b[2], a[3]]
+            g, h = more
+            pre = [a[1], b[1], a[2], c[1], d[1]] + [t[0] for t in panel_tasks] + [keep, b[2], a[3]]
             plan = {
-                (0, 1): [c[2], d[2]],
+                (0, 1): [c[2], d[2], e[1]],
                 (0, 2): [b[3]],
-                (1, 0): [c[3], e[1]],
-                (1, 1): [d[3]],
-                (2, 1): [f[1]] + [t[1] for t in panel_tasks],
-                (3, 0): [e[2]],
-                (3, 1): [e[3]] + [t[2] for t in panel_tasks],
+                (1, 0): [c[3], f[1]],
+                (1, 1): [d[3], g[1]],
+                (1, 2): [h[1], e[2]],
+                (2, 1): [f[2], e[3]] + [t[1] for t in panel_tasks],
+                (2, 2): [g[2]],
+                (3, 0): [f[3]],
+                (3, 1): [h[2], g[3]],
             }
-            after = [f[2], f[3]]
+            after = [h[3]]
+            finally_ = [t[2] for t in panel_tasks]
         elif level == 2:
-            pre += [a[1], b[1], c[1], d[1], a[2], b[2], c[2], d[2], a[3], b[3], a[4]]
+            g, h = more
+            pre = [a[1], b[1], c[1], d[1], keep, a[2], b[2], c[2], d[2], e[1], f[1]]
+            pre += [a[3], b[3], a[4]]
             plan = {
-                (0, 1): [c[3], d[3]] + both(1),
+                (0, 1): [c[3], d[3], g[1], h[1]],
                 (0, 2): [b[4]],
-                (1, 0): [c[4]],
+                (1, 0): [c[4], e[2], f[2]],
                 (1, 1): [d[4]],
-                (2, 0): both(2),
-                (3, 1): [e[3]],
-                (3, 2): [e[4]],
+                (1, 2): [g[2], h[2], e[3]],
+                (2, 1): [f[3], e[4]],
+                (3, 0): [g[3]],
+                (3, 1): [f[4], h[3]],
+                (3, 2): [g[4]],
             }
-            after = [f[3], f[4]]
+            after = [h[4]]
         else:
-            inbox0, middle0, final0, inbox1, middle1, final1, sums0, sums1 = [take() for _ in range(8)]
+            extra, inbox0, middle0, final0, inbox1, middle1, final1, sums0, sums1 = [
+                take() for _ in range(9)
+            ]
             half = below // 2
             x = extra_task(links, (0, 1), extra, pl.ds(0, half), inbox0, middle0, final0, sums0)
             y = extra_task(links, (1, 0), extra, pl.ds(half, half), inbox1, middle1, final1, sums1)
-            pre += [a[1], b[1], c[1], d[1], a[2], b[2], c[2], d[2]] + both(1) + [x[0], y[0]]
+
+            def begin_extra():
+                height = result.shape[0]
+                rows = [None] * group
+                for index in range(group):
+                    start = pl.multiple_of(order + (index * row_count + row) * height, 8)
+                    rows[bit_reversed(index, LEVELS - 1)] = placed[pl.ds(start, height)]
+                part = halves(jnp.concatenate(rows, axis=0))
+                for left, task in ((0, x), (half, y)):
+                    other = halves(placed[order + left : order + left + half])
+                    value = -dot_split(part, other)
+                    extra[..., left : left + half] = value.reshape(*extra.shape[:3], half)
+                    task[0]()
+
+            pre = [a[1], b[1], c[1], d[1], begin_extra, a[2], b[2], c[2], d[2]] + both(1)
             pre += [a[3], b[3], a[4], c[3], d[3], b[4], a[5]]
             plan = {
                 (0, 1): both(2) + [c[4], d[4]],
@@ -518,15 +578,12 @@
         for action in pre:
             action()
 
-        count = order // BLOCK
-
         def diagonal(j):
-            place = j * count - j * (j - 1) // 2
-            return packed[pl.ds(pl.multiple_of(place * BLOCK, BLOCK), BLOCK)]
+            return packed[j * count - j * (j - 1) // 2]
 
         def column(j):
-            place = j * count - j * (j - 1) // 2 - j
-            return packed[pl.ds(pl.multiple_of(place * BLOCK, BLOCK), order)]
+            start = j * count - j * (j - 1) // 2 - j
+            return packed[pl.ds(start, count)].reshape(order, BLOCK)
 
     def hook(j, slot):
         for (when, which), actions in plan.items():
@@ -551,73 +608,28 @@
         result[:, half:] = sums1[...] - rest[:, half:]
         return
     width = order // group
+    blocks = below // BLOCK
     if first:
         for left in range(0, order, 2 * BLOCK):
             right = min(left + 2 * BLOCK, order)
             part = inverse[0, left:right, :right], inverse[1, left:right, :right]
-            result[:, left:right] = dot_split(halves(gathered[order:, :right]), part)
+            value = dot_split(halves(gathered[order:, :right]), part)
+            result[:blocks, :, left:right] = value.reshape(blocks, BLOCK, right - left)
     else:
         span = pl.ds(pl.multiple_of(member * width, BLOCK), width)
-        result[...] = dot_split(halves(columns[...]), (inverse[0, span], inverse[1, span]))
+        value = dot_split(halves(columns[...]), (inverse[0, span], inverse[1, span]))
+        result[:blocks] = value.reshape(blocks, BLOCK, width)
+    result[blocks] = jnp.zeros((BLOCK, width), jnp.float32)
+    for action in finally_:
+        action()
     for buffer, target in zip(held, joined):
         target[...] = buffer[...]
 
 
-def share_kernel(level, row_count, front, order, *refs):
-    group = 2**level
-    below = front - order
-    refs = list(refs)
-    take = lambda: refs.pop(0)
-    inverse_map, next_panel, fresh = take(), take(), take()
-    old = take() if level else None
-    kept, pivot_out, below_out = take(), take(), take()
-    extra = take() if level == LEVELS - 2 else None
-    placed, whole_panel, everything = take(), take(), take()
-    row = lax.axis_index("row")
-    depth = 0 if old is None else old.shape[1]
-    width = order // group
-    if old is not None:
-        kept[:below, :depth] = old[:below]
-    kept[:below, depth:] = fresh[...]
-    kept[below:] = jnp.zeros((BLOCK, depth + width), jnp.float32)
-    for i in range(front // BLOCK):
-        block = pl.multiple_of(inverse_map[i] * BLOCK, BLOCK)
-        placed[i * BLOCK : (i + 1) * BLOCK] = kept[pl.ds(block, BLOCK)]
-    held = next_panel.shape[0]
-    whole_panel[...] = jnp.zeros_like(whole_panel)
-    place = lax.axis_index("leaf") % (2 * group)
-    whole_panel[pl.ds(pl.multiple_of(place * held, 8), held)] = next_panel[...]
-    pivots = halves(placed[:order])
-    for t, (i, j) in enumerate(column_tiles(order)):
-        down = slice(i * BLOCK, (i + 1) * BLOCK)
-        along = slice(j * BLOCK, (j + 1) * BLOCK)
-        product = dot_split([p[down] for p in pivots], [p[along] for p in pivots])
-        everything[t * BLOCK : (t + 1) * BLOCK] = whole_panel[down, along] - product
-    for begin, end in pivot_chunks(order):
-        size = BLOCK // row_count
-        height = (end - begin) * size
-        mine = rows_at_scaled(height, begin * BLOCK, height)(row)
-        pivot_out[begin * size : end * size] = everything[mine]
-    height = below_out.shape[0]
-    mine = rows_at_scaled(height, order, height)(row)
-    below_out[...] = whole_panel[mine] - dot_split(halves(placed[mine]), pivots)
-    kept[:below] = placed[order:]
-    if level == LEVELS - 2:
-        top = 2 * group
-        height = below // (top * row_count)
-        for index in range(top):
-            start = pl.multiple_of(order + (index * row_count + row) * height, 8)
-            spot = bit_reversed(index, LEVELS - 1)
-            placed[spot * height : (spot + 1) * height] = placed[pl.ds(start, height)]
-        own_part = halves(placed[: top * height])
-        value = -dot_split(own_part, halves(kept[:below]))
-        extra[...] = value.reshape(extra.shape)
-
-
-def front_step(level, row_count, front, order, operands):
+def front_step(level, row_count, front, order, operands, panels):
     below = front - order
     width = order // 2**level
-    share = len(column_tiles(order)) * BLOCK // row_count
+    tiles = len(column_tiles(order))
     float32 = jnp.float32
 
     def vmem(*shape, dtype=float32):
@@ -640,24 +652,24 @@
         pltpu.SemaphoreType.DMA((copies,)),
         pltpu.SemaphoreType.DMA((copies,)),
     ]
-    panels = operands[1:] if level == 0 else operands[2:] if level == 1 else []
     heights = [row_count * panel.shape[0] for panel in panels]
     scratch += [vmem(height, order) for height in heights]
+    depth = sum(order // 2**k for k in range(level))
     if level == 0:
         scratch.append(vmem(front, order))
     else:
-        scratch += [
-            vmem(share * row_count, BLOCK),
-            vmem(level, share, BLOCK),
-            vmem(level, share, BLOCK),
-        ]
+        share = (tiles, BLOCK // row_count, BLOCK)
+        scratch += [vmem(tiles, BLOCK, BLOCK), vmem(*share), vmem(level, *share), vmem(level, *share)]
+        scratch.append(vmem(rest, order))
         if last:
             scratch += [vmem(2, level, rest // 4, order), vmem(2, level, rest // 4, order)]
         else:
             scratch += [vmem(level, rest, order), vmem(level, rest, order)]
+        scratch += [vmem(front, depth), vmem(front, order)]
     if last:
         height = rest // top
         half = below // 2
+        scratch.append(vmem(2, 2, 2 * height, below))
         for shape in ((1, 2), (2, 1)):
             scratch += [
                 vmem(*shape, 2 * height, half),
@@ -667,8 +679,15 @@
         scratch += [vmem(height, half), vmem(height, half)]
         shapes = out(height, below)
     else:
-        shapes = [out(below, width)] + [out(height, order) for height in heights]
+        blocks = below // BLOCK + 1
+        shapes = [out(blocks, BLOCK, width)]
+        if level:
+            shapes.append(out(blocks, BLOCK, depth))
+        shapes += [out(height, order) for height in heights]
+    operands = operands + panels
     specs = [pl.BlockSpec(memory_space=pltpu.VMEM)] * len(operands)
+    if level:
+        specs[0] = pl.BlockSpec(memory_space=pltpu.SMEM)
     return pl.pallas_call(
         functools.partial(front_kernel, level, row_count, front, order),
         out_shape=shapes,
@@ -681,34 +700,6 @@
     )(*operands)
 
 
-def share_step(level, row_count, front, order, operands):
-    below = front - order
-    depth = sum(order // 2**k for k in range(level + 1))
-    tiles = len(column_tiles(order))
-    rest = below // row_count
-
-    def out(*shape):
-        return jax.ShapeDtypeStruct(shape, jnp.float32)
-
-    shapes = [out(below + BLOCK, depth), out(tiles * BLOCK // row_count, BLOCK), out(rest, order)]
-    if level == LEVELS - 2:
-        shapes.append(out(2, 2, rest // 4, below))
-    specs = [pl.BlockSpec(memory_space=pltpu.VMEM)] * len(operands)
-    specs[0] = pl.BlockSpec(memory_space=pltpu.SMEM)
-    return pl.pallas_call(
-        functools.partial(share_kernel, level, row_count, front, order),
-        out_shape=shapes,
-        in_specs=specs,
-        scratch_shapes=[
-            pltpu.VMEM((front, depth), jnp.float32),
-            pltpu.VMEM((front, order), jnp.float32),
-            pltpu.VMEM((tiles * BLOCK, BLOCK), jnp.float32),
-        ],
-        name=f"share{level}",
-        compiler_params=pltpu.CompilerParams(vmem_limit_bytes=60 * 2**20),
-    )(*operands)
-
-
 def body(panel0, panel1, panel2, panel3, maps1, maps2, maps3):
     block_maps = (maps1, maps2, maps3)
     row_count = lax.axis_size("row")
@@ -717,23 +708,21 @@
     front = panel0.shape[0] * row_count
     parents = front // BLOCK
     children = (front - order) // BLOCK
-    operands = [panel0, panel1]
-    waiting = [[], [panel2, panel3], []]
-    old = []
+    operands = [panel0]
+    waiting = [[panel1], [panel2, panel3], [], []]
     panels = []
-    for level in range(LEVELS - 1):
+    for level in range(LEVELS):
+        outs = front_step(level, row_count, front, order, operands, waiting[level])
+        if level == LEVELS - 1:
+            return outs
         blocks = lax.dynamic_index_in_dim(block_maps[level], leaf // 2**level, 0, keepdims=False)
         hit = blocks[None, :] == jnp.arange(parents, dtype=jnp.int32)[:, None]
         back = jnp.min(
             jnp.where(hit, jnp.arange(children, dtype=jnp.int32)[None, :], children), axis=1
         )
-        fresh, *joined = front_step(level, row_count, front, order, operands + waiting[level])
-        panels += joined
-        shared = [back, panels[level], fresh] + old
-        outs = share_step(level, row_count, front, order, shared)
-        old = [outs[0]]
-        operands = list(outs[1:])
-    return front_step(LEVELS - 1, row_count, front, order, operands)
+        data = outs[: 2 if level else 1]
+        panels += outs[len(data) :]
+        operands = [back, panels[level], *data]
 
 
 def solution(mesh):

time: 206 us -> 190 us (0.922)
  Pallas kernels: 201 us -> 185 us
    pallas_call x3 -> x0, Pallas kernels: 22.5 us -> none  [share_step(): pl.pallas_call(functools.partial(share_kernel, level, row_count, front, o...]
    pallas_call x4, Pallas kernels: 179 us -> 185 us  [front_step(): pl.pallas_call(functools.partial(front_kernel, level, row_count, front, o...]
where the time goes in v1:
time: 190 us
  Pallas kernels  185 us (97%)
  local copies, waits for them, and re-layouts  2.96 us (2%)
    pallas_call x4, Pallas kernels, front_step(): pl.pallas_call(functools.partial(front_kernel, level, row_count, front, o...  185 us

profile of v1, /device:TPU:0, one launch (start us, length us, event | category | flops | bytes accessed | tf_op | source)
XLA Modules:
  0.0 189.7 jit_solution(4666054480542035932)
XLA Ops:
  0.0 0.0 copy-start
  0.0 0.7 fusion
  0.7 0.6 select_reduce_fusion.2.refs_0_
  1.3 0.7 fusion.2
  2.0 0.7 select_reduce_fusion.refs_0_
  2.7 0.0 copy-done
  2.7 0.6 select_reduce_fusion.1.refs_0_
  3.3 37.1 %front0.1 = (f32[9,128,512]{2,1,0:T(8,128)}, f32[768,512]{1,0:T(8,128)}) custom-call(f32[384,512]{1,0:T(8,128)} %refs_0_.1, f32[192,512]{1,0:T(8,128)} %refs_1_.1), custom_call_target="tpu_custom_call" | custom-call | tf_op jit(solution)/shard_map/front0/pallas_call | solution.py:691
  40.4 41.0 %front1.1 = (f32[9,128,256]{2,1,0:T(8,128)}, f32[9,128,512]{2,1,0:T(8,128)}, f32[384,512]{1,0:T(8,128)}, f32[192,512]{1,0:T(8,128)}) custom-call(s32[12]{0:T(128)} %select_reduce_fusion.1.refs_0_, f32[768,512]{1,0:T(8,128)} %get-tuple-element.13.refs_1_, f32[9,128,512]{2,1,0:T(8,128)} %get-tuple-element.14.refs_2_, f32[96,512]{1,0:T(8,128)} %refs_3_.1, ...), custom_call_target="tpu_custom_call" | custom-call | tf_op jit(solution)/shard_map/front1/pallas_call | solution.py:691
  81.4 44.3 %front2.1 = (f32[9,128,128]{2,1,0:T(8,128)}, f32[9,128,768]{2,1,0:T(8,128)}) custom-call(s32[12]{0:T(128)} %select_reduce_fusion.refs_0_, f32[384,512]{1,0:T(8,128)} %get-tuple-element.16.refs_1_, f32[9,128,256]{2,1,0:T(8,128)} %get-tuple-element.17.refs_2_, f32[9,128,512]{2,1,0:T(8,128)} %get-tuple-element.18.refs_3_), custom_call_target="tpu_custom_call" | custom-call | tf_op jit(solution)/shard_map/front2/pallas_call | solution.py:691
  125.7 62.4 %front3.1 = f32[32,1024]{1,0:T(8,128)} custom-call(s32[12]{0:T(128)} %select_reduce_fusion.2.refs_0_, f32[192,512]{1,0:T(8,128)} %get-tuple-element.15.refs_1_, f32[9,128,128]{2,1,0:T(8,128)} %get-tuple-element.19.refs_2_, f32[9,128,768]{2,1,0:T(8,128)} %get-tuple-element.20.refs_3_), custom_call_target="tpu_custom_call" | custom-call | tf_op jit(solution)/shard_map/front3/pallas_call | solution.py:691
  188.1 1.6 copy.9
  (1 shorter events, 0.0 us)
Async XLA Ops:
  0.0 2.7 %copy-start = (s32[8,8]{1,0:T(8,128)S(1)}, s32[8,8]{1,0:T(8,128)}, u32[]{:S(2)}) copy-start(s32[8,8]{1,0:T(8,128)} %param.11) | copy-start | bytes 772

commit v2 on v1

--- a/solution.py
+++ b/solution.py
@@ -39,7 +39,7 @@
     return jnp.broadcast_to(value, (rows, columns))
 
 
-def diagonal_inverse(block, pause):
+def diagonal_inverse(block, nothing, pause):
     count = BLOCK // SUB
     rows = [block[v * SUB : (v + 1) * SUB] for v in range(count)]
     lane = lax.broadcasted_iota(jnp.int32, (SUB, BLOCK), 1)
@@ -50,7 +50,9 @@
         base = b * SUB
         inside = (lane >= base) & (lane < base + SUB)
         own = rows[b]
-        columns = [spread(own[:, base + j : base + j + 1], SUB, BLOCK) for j in range(SUB)]
+        columns = [
+            spread(own[:, base + j : base + j + 1], SUB, BLOCK) + nothing for j in range(SUB)
+        ]
         a = [
             [spread(columns[j][i : i + 1], SUB, BLOCK) for j in range(i + 1)] for i in range(SUB)
         ]
@@ -334,7 +336,7 @@
 def factor(diagonal, column, lower, inverse, spare, hook):
     order = lower.shape[1]
     tiles = order // BLOCK
-    product, cross, block = spare
+    product, cross, block, zeros = spare
     row_ids = lax.broadcasted_iota(jnp.int32, (order, BLOCK), 0)
 
     def store(target, where, value):
@@ -350,7 +352,7 @@
         product[...] = dot_split((lower[0], lower[1]), mine)
         cross[...] = dot_split_nn(mine, (inverse[0], inverse[1]))
         block[...] = diagonal_inverse(
-            diagonal(j) - dot_split(mine, mine), functools.partial(hook, j, 1)
+            diagonal(j) - dot_split(mine, mine), zeros[...], functools.partial(hook, j, 1)
         )
         hook(j, 2)
         own = halves(block[...])
@@ -386,12 +388,14 @@
     if not first and not last:
         kept = take()
     joined = [take() for _ in panels]
-    lower, inverse, product, cross, block, columns, sends, receives = [take() for _ in range(8)]
+    lower, inverse, product, cross, block, zeros = [take() for _ in range(6)]
+    columns, sends, receives = [take() for _ in range(3)]
     held = [take() for _ in panels]
     near = neighbours(level)
     links = Links(near, sends, receives)
     lower[...] = jnp.zeros_like(lower)
     inverse[...] = jnp.zeros_like(inverse)
+    zeros[...] = jnp.zeros_like(zeros)
     panel_tasks = []
     for part, buffer in zip(panels, held):
         height = part.shape[0]
@@ -561,20 +565,20 @@
                     extra[..., left : left + half] = value.reshape(*extra.shape[:3], half)
                     task[0]()
 
-            pre = [a[1], b[1], c[1], d[1], begin_extra, a[2], b[2], c[2], d[2]] + both(1)
-            pre += [a[3], b[3], a[4], c[3], d[3], b[4], a[5]]
+            pre = [a[1], b[1], a[2], b[2], c[1], d[1]] + both(1) + [c[2], d[2], begin_extra]
+            pre += [a[3], b[3]] + both(2) + [a[4], c[3], d[3], b[4], a[5]]
             plan = {
-                (0, 1): both(2) + [c[4], d[4]],
+                (0, 1): both(3) + [c[4], d[4]],
                 (0, 2): [b[5]],
-                (1, 0): [c[5]] + both(3),
-                (1, 1): [x[1], y[1]] + both(4),
-                (2, 0): [d[5]] + both(5),
-                (2, 1): [x[2], y[2]],
-                (2, 2): both(6),
-                (3, 1): [x[3], y[3]],
-                (3, 2): [e[7]],
+                (1, 0): [c[5]] + both(4),
+                (1, 1): both(5),
+                (1, 2): both(6),
+                (2, 0): [d[5], x[1], y[1]],
+                (2, 2): [x[2], y[2]],
+                (3, 1): [e[7]],
+                (3, 2): [e[8]],
             }
-            after = [f[7], e[8], f[8]]
+            after = [x[3], y[3], f[7], f[8]]
         for action in pre:
             action()
 
@@ -594,7 +598,7 @@
                     for action in actions:
                         action()
 
-    factor(diagonal, column, lower, inverse, (product, cross, block), hook)
+    factor(diagonal, column, lower, inverse, (product, cross, block, zeros), hook)
     for action in after:
         action()
     if last:
@@ -648,6 +652,7 @@
         vmem(order, BLOCK),
         vmem(BLOCK, order),
         vmem(BLOCK, BLOCK),
+        vmem(SUB, BLOCK),
         vmem(below if level else 8, order),
         pltpu.SemaphoreType.DMA((copies,)),
         pltpu.SemaphoreType.DMA((copies,)),

time: 190 us -> 175 us (0.921)
  Pallas kernels: 185 us -> 170 us
    pallas_call x4, Pallas kernels: 185 us -> 170 us  [front_step(): pl.pallas_call(functools.partial(front_kernel, level, row_count, front, o...]
where the time goes in v2:
time: 175 us
  Pallas kernels  170 us (97%)
  local copies, waits for them, and re-layouts  2.96 us (2%)
  other arithmetic  1.86 us (1%)
    pallas_call x4, Pallas kernels, front_step(): pl.pallas_call(functools.partial(front_kernel, level, row_count, front, o...  170 us

profile of v2, /device:TPU:0, one launch (start us, length us, event | category | flops | bytes accessed | tf_op | source)
XLA Modules:
  0.0 174.9 jit_solution(1077039794129567935)
XLA Ops:
  0.0 0.0 copy-start
  0.0 0.7 fusion
  0.7 0.6 select_reduce_fusion.2.refs_0_
  1.3 0.7 fusion.2
  2.0 0.7 select_reduce_fusion.refs_0_
  2.7 0.0 copy-done
  2.7 0.6 select_reduce_fusion.1.refs_0_
  3.3 35.8 %front0.1 = (f32[9,128,512]{2,1,0:T(8,128)}, f32[768,512]{1,0:T(8,128)}) custom-call(f32[384,512]{1,0:T(8,128)} %refs_0_.1, f32[192,512]{1,0:T(8,128)} %refs_1_.1), custom_call_target="tpu_custom_call" | custom-call | tf_op jit(solution)/shard_map/front0/pallas_call | solution.py:696
  39.1 38.5 %front1.1 = (f32[9,128,256]{2,1,0:T(8,128)}, f32[9,128,512]{2,1,0:T(8,128)}, f32[384,512]{1,0:T(8,128)}, f32[192,512]{1,0:T(8,128)}) custom-call(s32[12]{0:T(128)} %select_reduce_fusion.1.refs_0_, f32[768,512]{1,0:T(8,128)} %get-tuple-element.13.refs_1_, f32[9,128,512]{2,1,0:T(8,128)} %get-tuple-element.14.refs_2_, f32[96,512]{1,0:T(8,128)} %refs_3_.1, ...), custom_call_target="tpu_custom_call" | custom-call | tf_op jit(solution)/shard_map/front1/pallas_call | solution.py:696
  77.6 41.7 %front2.1 = (f32[9,128,128]{2,1,0:T(8,128)}, f32[9,128,768]{2,1,0:T(8,128)}) custom-call(s32[12]{0:T(128)} %select_reduce_fusion.refs_0_, f32[384,512]{1,0:T(8,128)} %get-tuple-element.16.refs_1_, f32[9,128,256]{2,1,0:T(8,128)} %get-tuple-element.17.refs_2_, f32[9,128,512]{2,1,0:T(8,128)} %get-tuple-element.18.refs_3_), custom_call_target="tpu_custom_call" | custom-call | tf_op jit(solution)/shard_map/front2/pallas_call | solution.py:696
  119.3 54.0 %front3.1 = f32[32,1024]{1,0:T(8,128)} custom-call(s32[12]{0:T(128)} %select_reduce_fusion.2.refs_0_, f32[192,512]{1,0:T(8,128)} %get-tuple-element.15.refs_1_, f32[9,128,128]{2,1,0:T(8,128)} %get-tuple-element.19.refs_2_, f32[9,128,768]{2,1,0:T(8,128)} %get-tuple-element.20.refs_3_), custom_call_target="tpu_custom_call" | custom-call | tf_op jit(solution)/shard_map/front3/pallas_call | solution.py:696
  173.3 1.6 copy.9
  (1 shorter events, 0.0 us)
Async XLA Ops:
  0.0 2.7 %copy-start = (s32[8,8]{1,0:T(8,128)S(1)}, s32[8,8]{1,0:T(8,128)}, u32[]{:S(2)}) copy-start(s32[8,8]{1,0:T(8,128)} %param.11) | copy-start | bytes 772

commit v3 on v2

--- a/solution.py
+++ b/solution.py
@@ -185,7 +185,7 @@
     peers = partners + [sibling] + across
     for peer in peers:
         pl.semaphore_signal(barrier, inc=1, device_id=peer, device_id_type=pl.DeviceIdType.MESH)
-    pl.semaphore_wait(barrier, len(peers))
+    return functools.partial(pl.semaphore_wait, barrier, len(peers))
 
 
 def bit_reversed(index, bits):
@@ -393,6 +393,7 @@
     held = [take() for _ in panels]
     near = neighbours(level)
     links = Links(near, sends, receives)
+    arrived = entry_barrier(near)
     lower[...] = jnp.zeros_like(lower)
     inverse[...] = jnp.zeros_like(inverse)
     zeros[...] = jnp.zeros_like(zeros)
@@ -402,7 +403,7 @@
         panel_tasks.append(gather_task(links.gather(buffer, rows_at(height), part)))
         buffer[rows_at(height)(row)] = part[...]
     if first:
-        entry_barrier(near)
+        arrived()
         gathered = take()
         chunk = panel.shape[0]
 
@@ -492,7 +493,6 @@
         whole_panel[pl.ds(pl.multiple_of(member * held_rows, 8), held_rows)] = next_panel[...]
         for i in range(front // BLOCK):
             fetch(i)
-        entry_barrier(near)
         pivots = halves(placed[:order])
         mine = [pl.ds(pl.multiple_of(i * BLOCK + row * size, 8), size) for i in range(count)]
         own = halves(jnp.concatenate([placed[span] for span in mine], axis=0))
@@ -500,6 +500,7 @@
         for t, (i, j) in enumerate(column_tiles(order)):
             along = slice(j * BLOCK, (j + 1) * BLOCK)
             pivot_share[t] = whole_panel[mine[i], along] - part[i * size : (i + 1) * size, along]
+        arrived()
         for task in (a, b, c, d):
             task[0]()
         spot = rows_at_scaled(share, order, share)(row)

time: 175 us -> 172 us (0.983)
  Pallas kernels: 170 us -> 167 us
    pallas_call x4, Pallas kernels: 170 us -> 167 us  [front_step(): pl.pallas_call(functools.partial(front_kernel, level, row_count, front, o...]
where the time goes in v3:
time: 172 us
  Pallas kernels  167 us (97%)
  local copies, waits for them, and re-layouts  2.96 us (2%)
  other arithmetic  1.86 us (1%)
    pallas_call x4, Pallas kernels, front_step(): pl.pallas_call(functools.partial(front_kernel, level, row_count, front, o...  167 us

profile of v3, /device:TPU:0, one launch (start us, length us, event | category | flops | bytes accessed | tf_op | source)
XLA Modules:
  0.0 171.8 jit_solution(483579390333621635)
XLA Ops:
  0.0 0.0 copy-start
  0.0 0.7 fusion
  0.7 0.6 select_reduce_fusion.2.refs_0_
  1.3 0.7 fusion.2
  2.0 0.7 select_reduce_fusion.refs_0_
  2.7 0.0 copy-done
  2.7 0.6 select_reduce_fusion.1.refs_0_
  3.3 35.7 %front0.1 = (f32[9,128,512]{2,1,0:T(8,128)}, f32[768,512]{1,0:T(8,128)}) custom-call(f32[384,512]{1,0:T(8,128)} %refs_0_.1, f32[192,512]{1,0:T(8,128)} %refs_1_.1), custom_call_target="tpu_custom_call" | custom-call | tf_op jit(solution)/shard_map/front0/pallas_call | solution.py:697
  38.9 37.5 %front1.1 = (f32[9,128,256]{2,1,0:T(8,128)}, f32[9,128,512]{2,1,0:T(8,128)}, f32[384,512]{1,0:T(8,128)}, f32[192,512]{1,0:T(8,128)}) custom-call(s32[12]{0:T(128)} %select_reduce_fusion.1.refs_0_, f32[768,512]{1,0:T(8,128)} %get-tuple-element.13.refs_1_, f32[9,128,512]{2,1,0:T(8,128)} %get-tuple-element.14.refs_2_, f32[96,512]{1,0:T(8,128)} %refs_3_.1, ...), custom_call_target="tpu_custom_call" | custom-call | tf_op jit(solution)/shard_map/front1/pallas_call | solution.py:697
  76.4 40.3 %front2.1 = (f32[9,128,128]{2,1,0:T(8,128)}, f32[9,128,768]{2,1,0:T(8,128)}) custom-call(s32[12]{0:T(128)} %select_reduce_fusion.refs_0_, f32[384,512]{1,0:T(8,128)} %get-tuple-element.16.refs_1_, f32[9,128,256]{2,1,0:T(8,128)} %get-tuple-element.17.refs_2_, f32[9,128,512]{2,1,0:T(8,128)} %get-tuple-element.18.refs_3_), custom_call_target="tpu_custom_call" | custom-call | tf_op jit(solution)/shard_map/front2/pallas_call | solution.py:697
  116.7 53.5 %front3.1 = f32[32,1024]{1,0:T(8,128)} custom-call(s32[12]{0:T(128)} %select_reduce_fusion.2.refs_0_, f32[192,512]{1,0:T(8,128)} %get-tuple-element.15.refs_1_, f32[9,128,128]{2,1,0:T(8,128)} %get-tuple-element.19.refs_2_, f32[9,128,768]{2,1,0:T(8,128)} %get-tuple-element.20.refs_3_), custom_call_target="tpu_custom_call" | custom-call | tf_op jit(solution)/shard_map/front3/pallas_call | solution.py:697
  170.2 1.6 copy.9
  (1 shorter events, 0.0 us)
Async XLA Ops:
  0.0 2.7 %copy-start = (s32[8,8]{1,0:T(8,128)S(1)}, s32[8,8]{1,0:T(8,128)}, u32[]{:S(2)}) copy-start(s32[8,8]{1,0:T(8,128)} %param.11) | copy-start | bytes 772
